TPU v7x, 32 devices: a whole 2x2x4 slice. The times are simulated.
32 devices in a mesh: seq: 8 (over y, x, core), mp: 4 (over z).
Axes of the slice: x: 2, y: 2, z: 4, core: 2. Of those that a mesh axis runs over, the one named last changes fastest.
Arguments:
- stream: float32 [4096, 2048], P('seq', 'mp'), may hold values from -6 to 6
- doc_starts: int32 [4096], P('seq'), may hold values 0 or 1
- gain_first: float32 [2048], replicated, may hold values from 0.5 to 1.5
- proj_inner: bfloat16 [2048, 2560], P(None, 'mp'), may hold values from -0.125 to 0.125
- proj_gate: bfloat16 [2048, 2560], P(None, 'mp'), may hold values from -0.125 to 0.125
- conv_weight: float32 [4, 2560], P(None, 'mp'), may hold values from -3 to 3
- conv_bias: float32 [2560], P('mp'), may hold values from -3 to 3
- gate_recur: bfloat16 [16, 160, 160], P('mp'), may hold values from -0.5 to 0.5
- gate_input: bfloat16 [16, 160, 160], P('mp'), may hold values from -0.5 to 0.5
- bias_recur: float32 [2560], P('mp'), may hold values from -3 to 3
- bias_input: float32 [2560], P('mp'), may hold values from -3 to 3
- decay_param: float32 [2560], P('mp'), may hold values from 3.4 to 15, as said below
- proj_out: bfloat16 [2560, 2048], P('mp'), may hold values from -0.25 to 0.25
- gain_second: float32 [2048], replicated, may hold values from 0.5 to 1.5
- mlp_gate: bfloat16 [2048, 6144], P(None, 'mp'), may hold values from -0.125 to 0.125
- mlp_up: bfloat16 [2048, 6144], P(None, 'mp'), may hold values from -0.125 to 0.125
- mlp_down: bfloat16 [6144, 2048], P('mp'), may hold values from -0.15625 to 0.15625
- cotangent: float32 [4096, 2048], P('seq', 'mp'), may hold values from -6 to 6
Outputs:
- output: float32 [4096, 2048], P('seq', 'mp')
- grad_stream: float32 [4096, 2048], P('seq', 'mp')
- grad_gain_first: float32 [2048], replicated
- grad_proj_inner: float32 [2048, 2560], P('seq', 'mp')
- grad_proj_gate: float32 [2048, 2560], P('seq', 'mp')
- grad_conv_weight: float32 [4, 2560], P(None, 'mp')
- grad_conv_bias: float32 [2560], P('mp')
- grad_gate_recur: float32 [16, 160, 160], P('mp')
- grad_gate_input: float32 [16, 160, 160], P('mp')
- grad_bias_recur: float32 [2560], P('mp')
- grad_bias_input: float32 [2560], P('mp')
- grad_decay: float32 [2560], P('mp')
- grad_proj_out: float32 [2560, 2048], P(('mp', 'seq'))
- grad_gain_second: float32 [2048], replicated
- grad_mlp_gate: float32 [2048, 6144], P('seq', 'mp')
- grad_mlp_up: float32 [2048, 6144], P('seq', 'mp')
- grad_mlp_down: float32 [6144, 2048], P(('mp', 'seq'))
Inputs may be any that keep to these rules, and one draw needn't show every extreme that they name: decay_param is -log(exp(q) - 1) for a per-channel rate q between 0.05 / 4096 and 0.03. `doc_starts`: a 1 marks the first token of a document.
All inputs are finite; a program needn't handle non-finite values. No bound on the sum of `doc_starts` on one device may be relied on, other than what follows from the above.
Results may differ from a plain program's by a relative error of at most 0.0089.
Values sent between devices are 32-bit elements; how exact they have to be, the bound alone decides.
No kernel may reach another device: no remote copies, remote signals or barrier semaphores. Data moves between devices by JAX's collectives and lax.ppermute only.
A program may use at most 256 MiB of HBM per device.

v0:
```python
from functools import partial
import jax
import jax.numpy as jnp
from jax import lax
from jax.sharding import PartitionSpec as P

recur_scale = 8.0
norm_eps = 1e-06


def passed_along(value, axis, steps):
    count = lax.axis_size(axis)
    first, last = (max(0, -steps), min(count, count - steps))
    return lax.ppermute(value, axis, [(source, source + steps) for source in range(first, last)])


def carried_in(value, axis, join, neutral, backward):
    count, mine = (lax.axis_size(axis), lax.axis_index(axis))
    pieces = jax.tree.map(lambda part: lax.all_gather(part, axis), value)
    if backward:
        pieces = jax.tree.map(lambda part: part[::-1], pieces)
        mine = count - 1 - mine
    running = jax.tree.map(
        lambda part, zero: jnp.full_like(part, 0) + jnp.asarray(zero, part.dtype), value, neutral
    )

    def turn(position, running):
        longer = join(running, jax.tree.map(lambda part: part[position], pieces))
        return jax.tree.map(lambda new, old: jnp.where(position < mine, new, old), longer, running)

    return lax.fori_loop(0, count - 1, turn, running)


def norm_rows(rows, gain):
    return rows * lax.rsqrt(jnp.mean(rows * rows, axis=-1, keepdims=True) + norm_eps) * gain


def matmul(left, right):
    return jnp.dot(left, right, preferred_element_type=jnp.float32)


def matmul_nt(left, right):
    return lax.dot_general(
        left, right, (((1,), (1,)), ((), ())), preferred_element_type=jnp.float32
    )


def matmul_tn(left, right):
    return lax.dot_general(
        left, right, (((0,), (0,)), ((), ())), preferred_element_type=jnp.float32
    )


def block_apply(values, weights):
    count = values.shape[0]
    groups = weights.shape[0]
    width = weights.shape[1]
    split = values.reshape(count, groups, width)
    mixed = jnp.einsum("tbi,bio->tbo", split, weights, preferred_element_type=jnp.float32)
    return mixed.reshape(count, groups * width)


def block_back(grads, weights):
    count = grads.shape[0]
    groups = weights.shape[0]
    width = weights.shape[1]
    split = grads.reshape(count, groups, width)
    mixed = jnp.einsum("tbo,bio->tbi", split, weights, preferred_element_type=jnp.float32)
    return mixed.reshape(count, groups * width)


def block_grad(values, grads, groups):
    count = values.shape[0]
    width = values.shape[1] // groups
    left = values.reshape(count, groups, width)
    right = grads.reshape(count, groups, width)
    return jnp.einsum("tbi,tbo->bio", left, right, preferred_element_type=jnp.float32)


def link(earlier, later):
    return (later[0] * earlier[0], later[0] * earlier[1] + later[1])


def local_scan(starts, conv_out, recur_pre, input_pre, decay):
    recur = jax.nn.sigmoid(recur_pre)
    entry = jax.nn.sigmoid(input_pre)
    log_decay = -recur_scale * recur * jax.nn.softplus(-decay)
    factor = starts + (1.0 - starts) * jnp.sqrt(-jnp.expm1(2.0 * log_decay))
    carry = jnp.exp(log_decay) * (1.0 - starts)
    fresh = factor * entry * conv_out
    return lax.associative_scan(link, (carry, fresh), axis=0)


def body(
    stream,
    doc_starts,
    gain_first,
    proj_inner,
    proj_gate,
    conv_weight,
    conv_bias,
    gate_recur,
    gate_input,
    bias_recur,
    bias_input,
    decay_param,
    proj_out,
    gain_second,
    mlp_gate,
    mlp_up,
    mlp_down,
    cotangent,
):
    count = stream.shape[0]
    own_width = stream.shape[1]
    inner_width = proj_inner.shape[1]
    ffn_width = mlp_gate.shape[1]
    groups = gate_recur.shape[0]
    lag = conv_weight.shape[0] - 1
    column = lax.axis_index("mp") * own_width
    rows_full = lax.all_gather(stream, "mp", axis=1, tiled=True)
    first_norm, first_back = jax.vjp(norm_rows, rows_full, gain_first)
    first_low = first_norm.astype(jnp.bfloat16)
    inner = matmul(first_low, proj_inner)
    gate_pre = matmul(first_low, proj_gate)
    starts = doc_starts.astype(jnp.float32)[:, None]
    keep = 1.0 - starts
    tail_keep = jnp.concatenate([keep[count - lag + 1 :], jnp.ones((1, 1), jnp.float32)], 0)
    tail_mask = jnp.flip(jnp.cumprod(jnp.flip(tail_keep, 0), 0), 0)
    prior = passed_along(inner[count - lag :] * tail_mask, "seq", 1)
    ext_inner = jnp.concatenate([prior, inner], 0)
    ext_keep = jnp.concatenate([jnp.ones((lag, 1), jnp.float32), keep], 0)
    valid = jnp.ones((count, 1), jnp.float32)
    valids = []
    conv_out = conv_weight[0] * inner
    for k in range(1, lag + 1):
        valid = valid * ext_keep[lag - k + 1 : lag - k + 1 + count]
        valids.append(valid)
        conv_out = conv_out + conv_weight[k] * ext_inner[lag - k : lag - k + count] * valid
    conv_out = conv_out + conv_bias
    conv_low = conv_out.astype(jnp.bfloat16)
    recur_pre = block_apply(conv_low, gate_recur) + bias_recur
    input_pre = block_apply(conv_low, gate_input) + bias_input
    scan_fn = partial(local_scan, starts)
    (span, partial_state), scan_back = jax.vjp(scan_fn, conv_out, recur_pre, input_pre, decay_param)
    identity = (jnp.ones((inner_width,), jnp.float32), jnp.zeros((inner_width,), jnp.float32))
    entering = carried_in(
        (span[count - 1], partial_state[count - 1]), "seq", link, identity, False
    )[1]
    states = span * entering + partial_state
    gated, gelu_back = jax.vjp(jax.nn.gelu, gate_pre)
    mixed_low = (gated * states).astype(jnp.bfloat16)
    branch = lax.psum(matmul(mixed_low, proj_out), "mp")
    resid = rows_full + branch
    second_norm, second_back = jax.vjp(norm_rows, resid, gain_second)
    second_low = second_norm.astype(jnp.bfloat16)
    ffn_gate = matmul(second_low, mlp_gate)
    ffn_up = matmul(second_low, mlp_up)
    ffn_act, act_back = jax.vjp(jax.nn.gelu, ffn_gate)
    hidden_low = (ffn_act * ffn_up).astype(jnp.bfloat16)
    mlp_own = lax.psum_scatter(matmul(hidden_low, mlp_down), "mp", scatter_dimension=1, tiled=True)
    output = lax.dynamic_slice_in_dim(resid, column, own_width, 1) + mlp_own
    cot_full = lax.all_gather(cotangent, "mp", axis=1, tiled=True)
    cot_low = cot_full.astype(jnp.bfloat16)
    d_hidden = matmul_nt(cot_low, mlp_down)
    d_gate_ffn = act_back(d_hidden * ffn_up)[0]
    d_pair_low = jnp.concatenate([d_gate_ffn, d_hidden * ffn_act], 1).astype(jnp.bfloat16)
    d_second_part = matmul_nt(d_pair_low[:, :ffn_width], mlp_gate) + matmul_nt(
        d_pair_low[:, ffn_width:], mlp_up
    )
    d_second = lax.psum(d_second_part, "mp")
    d_resid_norm, d_gain_second = second_back(d_second)
    d_resid = cot_full + d_resid_norm
    branch_low = d_resid.astype(jnp.bfloat16)
    d_mixed = matmul_nt(branch_low, proj_out)
    d_states = d_mixed * gated
    d_gate_low = gelu_back(d_mixed * states)[0].astype(jnp.bfloat16)
    outgoing = jnp.sum(d_states * span, axis=0)
    incoming = carried_in((span[count - 1], outgoing), "seq", link, identity, True)[1]
    d_total = d_states.at[count - 1].add(incoming)
    d_conv_direct, d_recur, d_input, d_decay = scan_back((d_total * entering, d_total))
    d_recur_low = d_recur.astype(jnp.bfloat16)
    d_input_low = d_input.astype(jnp.bfloat16)
    d_conv = (
        d_conv_direct + block_back(d_recur_low, gate_recur) + block_back(d_input_low, gate_input)
    )
    grad_gate_recur = block_grad(conv_low, d_recur_low, groups)
    grad_gate_input = block_grad(conv_low, d_input_low, groups)
    grad_bias_recur = jnp.sum(d_recur_low.astype(jnp.float32), axis=0)
    grad_bias_input = jnp.sum(d_input_low.astype(jnp.float32), axis=0)
    ext_grad = (
        jnp.zeros((count + lag, inner_width), jnp.float32).at[lag:].add(conv_weight[0] * d_conv)
    )
    conv_terms = [jnp.sum(d_conv * inner, axis=0)]
    for k in range(1, lag + 1):
        weighted = d_conv * valids[k - 1]
        ext_grad = ext_grad.at[lag - k : lag - k + count].add(conv_weight[k] * weighted)
        conv_terms.append(jnp.sum(weighted * ext_inner[lag - k : lag - k + count], axis=0))
    grad_conv_weight = jnp.stack(conv_terms, 0)
    grad_conv_bias = jnp.sum(d_conv, axis=0)
    returned = passed_along(ext_grad[:lag], "seq", -1)
    d_inner = ext_grad[lag:].at[count - lag :].add(returned * tail_mask)
    d_inner_low = d_inner.astype(jnp.bfloat16)
    first_pair_low = jnp.concatenate([d_inner_low, d_gate_low], 1)
    d_first_part = matmul_nt(d_inner_low, proj_inner) + matmul_nt(d_gate_low, proj_gate)
    d_first = lax.psum(d_first_part, "mp")
    d_rows_norm, d_gain_first = first_back(d_first)
    grad_stream = lax.dynamic_slice_in_dim(d_resid + d_rows_norm, column, own_width, 1)
    small = lax.psum(
        (
            d_gain_first,
            d_gain_second,
            grad_conv_weight,
            grad_conv_bias,
            grad_gate_recur,
            grad_gate_input,
            grad_bias_recur,
            grad_bias_input,
            d_decay,
        ),
        "seq",
    )
    grad_first, grad_out, grad_pair, grad_down = (
        lax.psum_scatter(
            matmul_tn(first_low, first_pair_low), "seq", scatter_dimension=0, tiled=True
        ),
        lax.psum_scatter(matmul_tn(mixed_low, branch_low), "seq", scatter_dimension=0, tiled=True),
        lax.psum_scatter(matmul_tn(second_low, d_pair_low), "seq", scatter_dimension=0, tiled=True),
        lax.psum_scatter(matmul_tn(hidden_low, cot_low), "seq", scatter_dimension=0, tiled=True),
    )
    return (
        output,
        grad_stream,
        small[0],
        grad_first[:, :inner_width],
        grad_first[:, inner_width:],
        small[2],
        small[3],
        small[4],
        small[5],
        small[6],
        small[7],
        small[8],
        grad_out,
        small[1],
        grad_pair[:, :ffn_width],
        grad_pair[:, ffn_width:],
        grad_down,
    )


def solution(mesh):
    in_specs = (
        P("seq", "mp"),
        P("seq"),
        P(),
        P(None, "mp"),
        P(None, "mp"),
        P(None, "mp"),
        P("mp"),
        P("mp", None, None),
        P("mp", None, None),
        P("mp"),
        P("mp"),
        P("mp"),
        P("mp", None),
        P(),
        P(None, "mp"),
        P(None, "mp"),
        P("mp", None),
        P("seq", "mp"),
    )
    out_specs = (
        P("seq", "mp"),
        P("seq", "mp"),
        P(),
        P("seq", "mp"),
        P("seq", "mp"),
        P(None, "mp"),
        P("mp"),
        P("mp", None, None),
        P("mp", None, None),
        P("mp"),
        P("mp"),
        P("mp"),
        P(("mp", "seq"), None),
        P(),
        P("seq", "mp"),
        P("seq", "mp"),
        P(("mp", "seq"), None),
    )
    return jax.shard_map(body, mesh=mesh, in_specs=in_specs, out_specs=out_specs, check_vma=False)
```

profile of v0, /device:TPU:0, one launch (start us, length us, event | category | flops | bytes accessed | tf_op | source)
XLA Modules:
  0.0 1586.7 jit_solution(3280703168751612168)
XLA Ops:
  10.0 83.1 %all-gather.7.cloned.1.call-done = f32[512,2048]{1,0:T(8,128)} async-done(((f32[512,512]{1,0:T(8,128)}), f32[512,2048]{1,0:T(8,128)}) %all-gather.7.cloned.1.call-update) | async-done | bytes 4194320 | tf_op jit(solution)/shard_map/all_gather | solution.py:121
  240.2 12.3 all-gather.2
  260.7 8.2 all-gather.1
  275.2 7.2 multiply_convert_fusion.4
  287.9 152.0 %all-reduce.129.cloned.1.call-done = f32[512,2048]{1,0:T(8,128)} async-done(((f32[512,2048]{1,0:T(8,128)}), f32[512,2048]{1,0:T(8,128)}) %all-reduce.129.cloned.1.call-update) | async-done | bytes 4194320 | tf_op jit(solution)/shard_map/psum | solution.py:153
  446.0 10.0 fusion.115
  461.1 60.2 %all-gather.9.cloned.1.call-done = f32[512,2048]{1,0:T(8,128)} async-done(((f32[512,512]{1,0:T(8,128)}), f32[512,2048]{1,0:T(8,128)}) %all-gather.9.cloned.1.call-update) | async-done | bytes 4194320 | tf_op jit(solution)/shard_map/all_gather | solution.py:163
  521.3 12.5 multiply_convert_fusion.2
  540.6 7.9 convolution_add_fusion.1
  551.2 9.5 fusion.116
  560.8 141.4 %all-reduce.131.cloned.1.call-done = f32[512,2048]{1,0:T(8,128)} async-done(((f32[512,2048]{1,0:T(8,128)}), f32[512,2048]{1,0:T(8,128)}) %all-reduce.131.cloned.1.call-update) | async-done | bytes 4194320 | tf_op jit(solution)/shard_map/psum | solution.py:171
  712.3 7.2 multiply_reduce_fusion.11
  719.5 9.0 all-gather.3
  952.4 6.8 convolution_add_fusion
  959.3 8.6 fusion.25
  968.0 14.3 fusion.8
  994.1 10.6 fusion.34
  1007.6 106.2 %all-reduce.133.cloned.1.call-done = f32[512,2048]{1,0:T(8,128)} async-done(((f32[512,2048]{1,0:T(8,128)}), f32[512,2048]{1,0:T(8,128)}) %all-reduce.133.cloned.1.call-update) | async-done | bytes 4194320 | tf_op jit(solution)/shard_map/psum | solution.py:206
  1120.2 25.1 %all-reduce.122 = (f32[2048]{0:T(1024)}, f32[4,640]{1,0:T(4,128)}, f32[640]{0:T(1024)}, f32[640]{0:T(1024)}, f32[640]{0:T(1024)}, /*index=5*/f32[640]{0:T(1024)}, f32[2048]{0:T(1024)}) all-reduce(f32[2048]{0:T(1024)S(1)} %get-tuple-element.317, f32[4,640]{1,0:T(4,128)S(1)} %pad_maximum_fusion.15, ...), channel_id=1, replica_groups=mesh['seq'=8,'mp'=4] {'seq'}, use_global_device_ids=true, to_apply=%region_15.16 | all-reduce | flops 9216 | bytes 73728 | tf_op jit(solution)/shard_map/psum | solution.py:209
  1148.4 49.5 %reduce-scatter.8.cloned.1.call-done = f32[256,1280]{1,0:T(8,128)} async-done(((f32[2048,1280]{1,0:T(8,128)}), f32[256,1280]{1,0:T(8,128)}) %reduce-scatter.8.cloned.1.call-update) | async-done | bytes 1310736 | tf_op jit(solution)/shard_map/reduce_scatter | solution.py:224
  1200.3 158.1 %reduce-scatter.12.cloned.1.call-done = f32[256,3072]{1,0:T(8,128)} async-done(((f32[2048,3072]{1,0:T(8,128)}), f32[256,3072]{1,0:T(8,128)}) %reduce-scatter.12.cloned.1.call-update) | async-done | bytes 3145744 | tf_op jit(solution)/shard_map/reduce_scatter | solution.py:228
  1362.1 58.5 %all-reduce.135.cloned.1.call-done = (f32[4,160,160]{2,1,0:T(8,128)}, f32[4,160,160]{2,1,0:T(8,128)}) async-done(((f32[4,160,160]{2,1,0:T(8,128)}, f32[4,160,160]{2,1,0:T(8,128)}), (f32[4,160,160]{2,1,0:T(8,128)}, f32[4,160,160]{2,1,0:T(8,128)})) %all-reduce.135.cloned.1.call-update) | async-done | bytes 819216 | tf_op jit(solution)/shard_map/psum | solution.py:209
  1420.6 60.0 %reduce-scatter.10.cloned.1.call-done = f32[80,2048]{1,0:T(8,128)} async-done(((f32[640,2048]{1,0:T(8,128)}), f32[80,2048]{1,0:T(8,128)}) %reduce-scatter.10.cloned.1.call-update) | async-done | bytes 655376 | tf_op jit(solution)/shard_map/reduce_scatter | solution.py:227
  1480.6 96.5 %reduce-scatter.14.cloned.1.call-done = f32[192,2048]{1,0:T(8,128)} async-done(((f32[1536,2048]{1,0:T(8,128)}), f32[192,2048]{1,0:T(8,128)}) %reduce-scatter.14.cloned.1.call-update) | async-done | bytes 1572880 | tf_op jit(solution)/shard_map/reduce_scatter | solution.py:229
  (818 shorter events, 466.3 us)
Async XLA Ops:
  7.2 268.0 %copy-start = (bf16[2048,640]{1,0:T(8,128)(2,1)S(1)}, bf16[2048,640]{1,0:T(8,128)(2,1)}, u32[]{:S(2)}) copy-start(bf16[2048,640]{1,0:T(8,128)(2,1)} %param.38) | copy-start | bytes 7864324
  7.2 85.9 %all-gather.7.cloned.1.call-start = ((), (), s32[]{:S(2)}) async-start(), calls=%async_computation.5 | async-start | bytes 5242880 | tf_op jit(solution)/shard_map/all_gather | solution.py:121
  7.9 431.9 %all-reduce.129.cloned.1.call-start = ((), (), s32[]{:S(2)}) async-start(), calls=%async_computation.6 | async-start | bytes 8388608 | tf_op jit(solution)/shard_map/psum | solution.py:153
  8.7 112.7 %copy-start.115 = (f32[512]{0:T(512)}, f32[512]{0:T(512)S(1)}, u32[]{:S(2)}) copy-start(f32[512]{0:T(512)S(1)} %broadcast_subtract_fusion) | copy-start | bytes 6148
  9.3 94.6 %copy-start.162 = (f32[512,1]{0,1:T(1,128)}, f32[512,1]{0,1:T(1,128)S(1)}, u32[]{:S(2)}) copy-start(f32[512,1]{0,1:T(1,128)S(1)} %get-tuple-element.400) | copy-start | bytes 6148
  10.0 111.4 %copy-start.117 = (f32[640]{0:T(1024)}, f32[640]{0:T(1024)S(1)}, u32[]{:S(2)}) copy-start(f32[640]{0:T(1024)S(1)} %broadcast_multiply_fusion.3) | copy-start | bytes 7684
  101.3 2.6 collective-permute-start
  287.1 234.3 %all-gather.9.cloned.1.call-start = ((), (), s32[]{:S(2)}) async-start(), calls=%async_computation.8 | async-start | bytes 5242880 | tf_op jit(solution)/shard_map/all_gather | solution.py:163
  287.8 156.1 %copy-start.129 = (f32[2048]{0:T(1024)S(1)}, f32[2048]{0:T(1024)}, u32[]{:S(2)}) copy-start(f32[2048]{0:T(1024)} %param.47) | copy-start | bytes 24580
  287.8 414.3 %all-reduce.131.cloned.1.call-start = ((), (), s32[]{:S(2)}) async-start(), calls=%async_computation.9 | async-start | bytes 8388608 | tf_op jit(solution)/shard_map/psum | solution.py:171
  548.5 456.3 %reduce-scatter.6.cloned.1.call-start = ((), (), s32[]{:S(2)}) async-start(), calls=%async_computation.7 | async-start | bytes 5242880 | tf_op jit(solution)/shard_map/reduce_scatter | solution.py:161
  560.7 141.5 %copy-start.170 = (f32[512]{0:T(512)S(1)}, f32[512]{0:T(512)}, u32[]{:S(2)}) copy-start(f32[512]{0:T(512)} %copy-done.169) | copy-start | bytes 6148
  560.7 553.0 %all-reduce.133.cloned.1.call-start = ((), (), s32[]{:S(2)}) async-start(), calls=%async_computation.10 | async-start | bytes 8388608 | tf_op jit(solution)/shard_map/psum | solution.py:206
  946.4 5.3 collective-permute-start.1
  959.3 238.6 %reduce-scatter.8.cloned.1.call-start = ((), (), s32[]{:S(2)}) async-start(), calls=%async_computation.11 | async-start | bytes 11796480 | tf_op jit(solution)/shard_map/reduce_scatter | solution.py:224
  967.9 390.5 %reduce-scatter.12.cloned.1.call-start = ((), (), s32[]{:S(2)}) async-start(), calls=%async_computation.13 | async-start | bytes 28311552 | tf_op jit(solution)/shard_map/reduce_scatter | solution.py:228
  982.3 438.3 %all-reduce.135.cloned.1.call-start = ((), (), s32[]{:S(2)}) async-start(), calls=%async_computation.15 | async-start | bytes 2621440 | tf_op jit(solution)/shard_map/psum | solution.py:209
  986.9 493.7 %reduce-scatter.10.cloned.1.call-start = ((), (), s32[]{:S(2)}) async-start(), calls=%async_computation.12 | async-start | bytes 5898240 | tf_op jit(solution)/shard_map/reduce_scatter | solution.py:227
  994.1 583.0 %reduce-scatter.14.cloned.1.call-start = ((), (), s32[]{:S(2)}) async-start(), calls=%async_computation.14 | async-start | bytes 14155776 | tf_op jit(solution)/shard_map/reduce_scatter | solution.py:229
  1004.8 108.9 %copy-start.159 = (f32[512]{0:T(512)S(1)}, f32[512]{0:T(512)}, u32[]{:S(2)}) copy-start(f32[512]{0:T(512)} %copy-done.158) | copy-start | bytes 6148
  1004.8 108.9 %copy-start.165 = (f32[2048]{0:T(1024)S(1)}, f32[2048]{0:T(1024)}, u32[]{:S(2)}) copy-start(f32[2048]{0:T(1024)} %param.36) | copy-start | bytes 24580
  1007.6 112.6 %copy-start.168 = (f32[2048]{0:T(1024)S(1)}, f32[2048]{0:T(1024)}, u32[]{:S(2)}) copy-start(f32[2048]{0:T(1024)} %get-tuple-element.315) | copy-start | bytes 24580
  1007.6 137.7 %copy-start.173 = (f32[512]{0:T(512)S(1)}, f32[512]{0:T(512)}, u32[]{:S(2)}) copy-start(f32[512]{0:T(512)} %copy-done.172) | copy-start | bytes 6148
  1420.6 158.5 %copy-start.72 = (f32[4,160,160]{2,1,0:T(8,128)S(1)}, f32[4,160,160]{2,1,0:T(8,128)}, u32[]{:S(2)}) copy-start(f32[4,160,160]{2,1,0:T(8,128)} %get-tuple-element.666) | copy-start | bytes 1228804
  (191 other events, 1186.1 us)
Sparse Core Ops, SparseCore 0:
  9.6 83.4 all-gather.6
  287.2 152.6 all-reduce.128
  441.5 79.7 all-gather.8
  548.6 153.4 all-reduce.130
  704.3 75.7 reduce-scatter.5
  959.4 154.2 all-reduce.132
  1117.2 80.5 reduce-scatter.7
  1201.5 156.8 reduce-scatter.11
  1362.8 57.8 all-reduce.134
  1424.8 55.7 reduce-scatter.9
  1484.7 92.3 reduce-scatter.13
where the time goes:
time: 1600 us; the launch traced here: 1590 us
  waiting for transfers between devices  967 us (60%)
  local copies, waits for them, and re-layouts  262 us (16%)
  other arithmetic  146 us (9%)
  matrix products  136 us (8%)
  blocking collectives  54.6 us (3%)
  between operations  16.9 us (1%)
    reduce_scatter x1, waiting for transfers between devices, body(): lax.psum_scatter(matmul_tn(second_low, d_pair_low), 'seq', scatter_dimens...  158 us
    psum x1, waiting for transfers between devices, body(): branch = lax.psum(matmul(mixed_low, proj_out), 'mp')  152 us
    psum x1, waiting for transfers between devices, body(): d_second = lax.psum(d_second_part, 'mp')  141 us
    pad x94, local copies, waits for them, and re-layouts, local_scan(): return lax.associative_scan(link, (carry, fresh), axis=0)  112 us
    psum x1, waiting for transfers between devices, body(): d_first = lax.psum(d_first_part, 'mp')  106 us
    reduce_scatter x1, waiting for transfers between devices, body(): lax.psum_scatter(matmul_tn(hidden_low, cot_low), 'seq', scatter_dimension...  96.5 us
    all_gather x1, waiting for transfers between devices, body(): rows_full = lax.all_gather(stream, 'mp', axis=1, tiled=True)  83.1 us
    slice x92, local copies, waits for them, and re-layouts, local_scan(): return lax.associative_scan(link, (carry, fresh), axis=0)  81.5 us
  transfers between devices with their start and end apart: 13, of which 11 were waited for; matrix products, arithmetic and copies ran while one was open for 21% of the time, Pallas kernels for 0%

commit v1 on v0

--- a/solution.py
+++ b/solution.py
@@ -203,7 +203,7 @@
     d_inner_low = d_inner.astype(jnp.bfloat16)
     first_pair_low = jnp.concatenate([d_inner_low, d_gate_low], 1)
     d_first_part = matmul_nt(d_inner_low, proj_inner) + matmul_nt(d_gate_low, proj_gate)
-    d_first = lax.psum(d_first_part, "mp")
+    d_first = jnp.sum(lax.all_gather(d_first_part, "mp"), axis=0)
     d_rows_norm, d_gain_first = first_back(d_first)
     grad_stream = lax.dynamic_slice_in_dim(d_resid + d_rows_norm, column, own_width, 1)
     small = lax.psum(

time: 1600 us -> 1730 us (1.081)
  waiting for transfers between devices: 967 us -> 1080 us
    all_gather x0 -> x1, waiting for transfers between devices: none -> 286 us  [body(): d_first = jnp.sum(lax.all_gather(d_first_part, 'mp'), axis=0)]
    psum x1 -> x0, waiting for transfers between devices: 106 us -> none  [body(): d_first = lax.psum(d_first_part, 'mp')]
    reduce_scatter x1, waiting for transfers between devices: 158 us -> 111 us  [body(): lax.psum_scatter(matmul_tn(second_low, d_pair_low), 'seq', scatter_dimens...]
  transfers between devices with their start and end apart: 13 -> 13, of which waited for: 11 -> 12; matrix products, arithmetic and copies ran while one was open for 21% -> 21% of each run, Pallas kernels for 0% -> 0%
where the time goes in v1:
time: 1730 us; the launch traced here: 1720 us
  waiting for transfers between devices  1080 us (62%)
  local copies, waits for them, and re-layouts  263 us (15%)
  other arithmetic  160 us (9%)
  matrix products  134 us (8%)
  blocking collectives  55.1 us (3%)
    all_gather x1, waiting for transfers between devices, body(): d_first = jnp.sum(lax.all_gather(d_first_part, 'mp'), axis=0)  286 us
    psum x1, waiting for transfers between devices, body(): branch = lax.psum(matmul(mixed_low, proj_out), 'mp')  152 us
    psum x1, waiting for transfers between devices, body(): d_second = lax.psum(d_second_part, 'mp')  141 us
    pad x94, local copies, waits for them, and re-layouts, local_scan(): return lax.associative_scan(link, (carry, fresh), axis=0)  112 us
    reduce_scatter x1, waiting for transfers between devices, body(): lax.psum_scatter(matmul_tn(second_low, d_pair_low), 'seq', scatter_dimens...  111 us
    reduce_scatter x1, waiting for transfers between devices, body(): lax.psum_scatter(matmul_tn(hidden_low, cot_low), 'seq', scatter_dimension...  96.9 us
    all_gather x1, waiting for transfers between devices, body(): rows_full = lax.all_gather(stream, 'mp', axis=1, tiled=True)  83.1 us
    slice x92, local copies, waits for them, and re-layouts, local_scan(): return lax.associative_scan(link, (carry, fresh), axis=0)  81.5 us
  transfers between devices with their start and end apart: 13, of which 12 were waited for; matrix products, arithmetic and copies ran while one was open for 21% of the time, Pallas kernels for 0%

profile of v1, /device:TPU:0, one launch (start us, length us, event | category | flops | bytes accessed | tf_op | source)
XLA Modules:
  0.0 1717.6 jit_solution(17833187085208074057)
XLA Ops:
  10.0 83.1 %all-gather.9.cloned.1.call-done = f32[512,2048]{1,0:T(8,128)} async-done(((f32[512,512]{1,0:T(8,128)}), f32[512,2048]{1,0:T(8,128)}) %all-gather.9.cloned.1.call-update) | async-done | bytes 4194320 | tf_op jit(solution)/shard_map/all_gather | solution.py:121
  240.3 12.3 all-gather.3
  260.8 8.2 all-gather.2
  275.3 7.2 multiply_convert_fusion.4
  288.0 152.0 %all-reduce.128.cloned.1.call-done = f32[512,2048]{1,0:T(8,128)} async-done(((f32[512,2048]{1,0:T(8,128)}), f32[512,2048]{1,0:T(8,128)}) %all-reduce.128.cloned.1.call-update) | async-done | bytes 4194320 | tf_op jit(solution)/shard_map/psum | solution.py:153
  446.1 10.0 fusion.115
  461.3 60.2 %all-gather.11.cloned.1.call-done = f32[512,2048]{1,0:T(8,128)} async-done(((f32[512,512]{1,0:T(8,128)}), f32[512,2048]{1,0:T(8,128)}) %all-gather.11.cloned.1.call-update) | async-done | bytes 4194320 | tf_op jit(solution)/shard_map/all_gather | solution.py:163
  521.4 12.7 multiply_convert_fusion.2
  540.9 7.9 convolution_add_fusion.1
  551.6 9.5 fusion.116
  561.1 141.4 %all-reduce.130.cloned.1.call-done = f32[512,2048]{1,0:T(8,128)} async-done(((f32[512,2048]{1,0:T(8,128)}), f32[512,2048]{1,0:T(8,128)}) %all-reduce.130.cloned.1.call-update) | async-done | bytes 4194320 | tf_op jit(solution)/shard_map/psum | solution.py:171
  719.8 9.0 all-gather.4
  950.8 8.5 fusion.25
  966.5 16.3 fusion.8
  994.6 10.7 fusion.34
  1008.1 33.1 %reduce-scatter.8.cloned.1.call-done = f32[256,1280]{1,0:T(8,128)} async-done(((f32[2048,1280]{1,0:T(8,128)}), f32[256,1280]{1,0:T(8,128)}) %reduce-scatter.8.cloned.1.call-update) | async-done | bytes 1310736 | tf_op jit(solution)/shard_map/reduce_scatter | solution.py:224
  1043.6 286.0 %all-gather.13.cloned.1.call-done = f32[2048,2048]{1,0:T(8,128)} async-done(((f32[512,2048]{1,0:T(8,128)}), f32[2048,2048]{1,0:T(8,128)}) %all-gather.13.cloned.1.call-update) | async-done | bytes 16777232 | tf_op jit(solution)/shard_map/all_gather | solution.py:206
  1329.7 10.3 reduce_sum.168
  1340.0 9.0 multiply_reduce_fusion.1
  1349.0 25.6 %all-reduce.122 = (f32[2048]{0:T(1024)}, f32[4,640]{1,0:T(4,128)}, f32[640]{0:T(1024)}, f32[640]{0:T(1024)}, f32[640]{0:T(1024)}, /*index=5*/f32[640]{0:T(1024)}, f32[2048]{0:T(1024)}) all-reduce(f32[2048]{0:T(1024)S(1)} %get-tuple-element.317, f32[4,640]{1,0:T(4,128)S(1)} %pad_maximum_fusion.15, ...), channel_id=1, replica_groups=mesh['seq'=8,'mp'=4] {'seq'}, use_global_device_ids=true, to_apply=%region_15.16 | all-reduce | flops 9216 | bytes 73728 | tf_op jit(solution)/shard_map/psum | solution.py:209
  1378.0 110.8 %reduce-scatter.12.cloned.1.call-done = f32[256,3072]{1,0:T(8,128)} async-done(((f32[2048,3072]{1,0:T(8,128)}), f32[256,3072]{1,0:T(8,128)}) %reduce-scatter.12.cloned.1.call-update) | async-done | bytes 3145744 | tf_op jit(solution)/shard_map/reduce_scatter | solution.py:228
  1492.6 58.9 %all-reduce.132.cloned.1.call-done = (f32[4,160,160]{2,1,0:T(8,128)}, f32[4,160,160]{2,1,0:T(8,128)}) async-done(((f32[4,160,160]{2,1,0:T(8,128)}, f32[4,160,160]{2,1,0:T(8,128)}), (f32[4,160,160]{2,1,0:T(8,128)}, f32[4,160,160]{2,1,0:T(8,128)})) %all-reduce.132.cloned.1.call-update) | async-done | bytes 819216 | tf_op jit(solution)/shard_map/psum | solution.py:209
  1551.5 59.6 %reduce-scatter.10.cloned.1.call-done = f32[80,2048]{1,0:T(8,128)} async-done(((f32[640,2048]{1,0:T(8,128)}), f32[80,2048]{1,0:T(8,128)}) %reduce-scatter.10.cloned.1.call-update) | async-done | bytes 655376 | tf_op jit(solution)/shard_map/reduce_scatter | solution.py:227
  1611.1 96.9 %reduce-scatter.14.cloned.1.call-done = f32[192,2048]{1,0:T(8,128)} async-done(((f32[1536,2048]{1,0:T(8,128)}), f32[192,2048]{1,0:T(8,128)}) %reduce-scatter.14.cloned.1.call-update) | async-done | bytes 1572880 | tf_op jit(solution)/shard_map/reduce_scatter | solution.py:229
  (817 shorter events, 472.6 us)
Async XLA Ops:
  7.2 268.1 %copy-start = (bf16[2048,640]{1,0:T(8,128)(2,1)S(1)}, bf16[2048,640]{1,0:T(8,128)(2,1)}, u32[]{:S(2)}) copy-start(bf16[2048,640]{1,0:T(8,128)(2,1)} %param.38) | copy-start | bytes 7864324
  7.2 85.9 %all-gather.9.cloned.1.call-start = ((), (), s32[]{:S(2)}) async-start(), calls=%async_computation.5 | async-start | bytes 5242880 | tf_op jit(solution)/shard_map/all_gather | solution.py:121
  7.9 432.0 %all-reduce.128.cloned.1.call-start = ((), (), s32[]{:S(2)}) async-start(), calls=%async_computation.6 | async-start | bytes 8388608 | tf_op jit(solution)/shard_map/psum | solution.py:153
  8.7 112.7 %copy-start.115 = (f32[512]{0:T(512)}, f32[512]{0:T(512)S(1)}, u32[]{:S(2)}) copy-start(f32[512]{0:T(512)S(1)} %broadcast_subtract_fusion) | copy-start | bytes 6148
  9.2 90.9 %copy-start.180 = (f32[3,1]{0,1:T(1,128)}, f32[3,1]{0,1:T(1,128)S(1)}, u32[]{:S(2)}) copy-start(f32[3,1]{0,1:T(1,128)S(1)} %rev.14) | copy-start | bytes 40
  9.3 94.6 %copy-start.160 = (f32[512,1]{0,1:T(1,128)}, f32[512,1]{0,1:T(1,128)S(1)}, u32[]{:S(2)}) copy-start(f32[512,1]{0,1:T(1,128)S(1)} %get-tuple-element.399) | copy-start | bytes 6148
  9.3 94.6 %copy-start.162 = (f32[512,1]{0,1:T(1,128)}, f32[512,1]{0,1:T(1,128)S(1)}, u32[]{:S(2)}) copy-start(f32[512,1]{0,1:T(1,128)S(1)} %get-tuple-element.400) | copy-start | bytes 6148
  9.3 86.5 %copy-start.164 = (f32[2048]{0:T(1024)S(1)}, f32[2048]{0:T(1024)}, u32[]{:S(2)}) copy-start(f32[2048]{0:T(1024)} %param.36) | copy-start | bytes 24580
  10.0 111.4 %copy-start.117 = (f32[640]{0:T(1024)}, f32[640]{0:T(1024)S(1)}, u32[]{:S(2)}) copy-start(f32[640]{0:T(1024)S(1)} %broadcast_multiply_fusion.3) | copy-start | bytes 7684
  101.3 2.6 collective-permute-start
  287.2 234.2 %all-gather.11.cloned.1.call-start = ((), (), s32[]{:S(2)}) async-start(), calls=%async_computation.8 | async-start | bytes 5242880 | tf_op jit(solution)/shard_map/all_gather | solution.py:163
  287.9 156.1 %copy-start.129 = (f32[2048]{0:T(1024)S(1)}, f32[2048]{0:T(1024)}, u32[]{:S(2)}) copy-start(f32[2048]{0:T(1024)} %param.47) | copy-start | bytes 24580
  288.0 414.6 %all-reduce.130.cloned.1.call-start = ((), (), s32[]{:S(2)}) async-start(), calls=%async_computation.9 | async-start | bytes 8388608 | tf_op jit(solution)/shard_map/psum | solution.py:171
  548.8 456.6 %reduce-scatter.6.cloned.1.call-start = ((), (), s32[]{:S(2)}) async-start(), calls=%async_computation.7 | async-start | bytes 5242880 | tf_op jit(solution)/shard_map/reduce_scatter | solution.py:161
  561.1 141.5 %copy-start.170 = (f32[512]{0:T(512)S(1)}, f32[512]{0:T(512)}, u32[]{:S(2)}) copy-start(f32[512]{0:T(512)} %copy-done.169) | copy-start | bytes 6148
  561.1 480.1 %reduce-scatter.8.cloned.1.call-start = ((), (), s32[]{:S(2)}) async-start(), calls=%async_computation.10 | async-start | bytes 11796480 | tf_op jit(solution)/shard_map/reduce_scatter | solution.py:224
  946.8 3.1 collective-permute-start.1
  959.3 370.3 %all-gather.13.cloned.1.call-start = ((), (), s32[]{:S(2)}) async-start(), calls=%async_computation.14 | async-start | bytes 20971520 | tf_op jit(solution)/shard_map/all_gather | solution.py:206
  966.4 522.4 %reduce-scatter.12.cloned.1.call-start = ((), (), s32[]{:S(2)}) async-start(), calls=%async_computation.12 | async-start | bytes 28311552 | tf_op jit(solution)/shard_map/reduce_scatter | solution.py:228
  982.8 568.7 %all-reduce.132.cloned.1.call-start = ((), (), s32[]{:S(2)}) async-start(), calls=%async_computation.15 | async-start | bytes 2621440 | tf_op jit(solution)/shard_map/psum | solution.py:209
  987.4 623.7 %reduce-scatter.10.cloned.1.call-start = ((), (), s32[]{:S(2)}) async-start(), calls=%async_computation.11 | async-start | bytes 5898240 | tf_op jit(solution)/shard_map/reduce_scatter | solution.py:227
  994.6 713.4 %reduce-scatter.14.cloned.1.call-start = ((), (), s32[]{:S(2)}) async-start(), calls=%async_computation.13 | async-start | bytes 14155776 | tf_op jit(solution)/shard_map/reduce_scatter | solution.py:229
  1340.0 34.5 %copy-start.173 = (f32[512]{0:T(512)S(1)}, f32[512]{0:T(512)}, u32[]{:S(2)}) copy-start(f32[512]{0:T(512)} %copy-done.172) | copy-start | bytes 6148
  1551.5 158.5 %copy-start.72 = (f32[4,160,160]{2,1,0:T(8,128)S(1)}, f32[4,160,160]{2,1,0:T(8,128)}, u32[]{:S(2)}) copy-start(f32[4,160,160]{2,1,0:T(8,128)} %get-tuple-element.666) | copy-start | bytes 1228804
  (190 other events, 941.3 us)
Sparse Core Ops, SparseCore 0:
  9.6 83.4 all-gather.8
  287.3 152.6 all-reduce.127
  441.6 79.7 all-gather.10
  549.0 153.4 all-reduce.129
  704.6 75.7 reduce-scatter.5
  959.4 81.7 reduce-scatter.7
  1042.9 286.7 all-gather.12
  1333.7 155.0 reduce-scatter.11
  1493.5 57.9 all-reduce.131
  1555.3 55.7 reduce-scatter.9
  1615.6 92.3 reduce-scatter.13
